TPU v7x, 128 devices: a whole 4x4x4 slice. The times are simulated.
128 devices in a mesh: row: 4 (over x_lo, core), col: 8 (over x_hi, y), tm: 4 (over z).
Axes of the slice: x: 4 (x_hi: 2, x_lo: 2; x = x_hi * 2 + x_lo), y: 4, z: 4, core: 2. Of those that a mesh axis runs over, the one named last changes fastest.
Arguments:
- right_sides: bfloat16 [8, 256, 16384], P(None, 'tm', ('row', 'col')), may hold values from -6 to 6
- eigen_basis: bfloat16 [16384, 16384], P('row', 'col'), may hold values from -0.046875 to 0.046875
- space_values: float32 [16384], P('col'), may hold values from 0.02 to 4
- time_basis: bfloat16 [256, 256], replicated, may hold values from -0.375 to 0.375
- time_values: float32 [256], replicated, may hold values from 0.05 to 4
- noise_level: float32 [1], replicated, may hold values from 0.05 to 0.5
Outputs:
- solved: float32 [8, 256, 16384], P(None, 'tm', ('row', 'col'))
All inputs are finite; a program needn't handle non-finite values.
Results may differ from a plain program's by a relative error of at most 0.0037.
Values may be sent and summed in bfloat16 or wider, within the bound.
No kernel may reach another device: no remote copies, remote signals or barrier semaphores. Data moves between devices by JAX's collectives and lax.ppermute only.
A program may use at most 128 MiB of HBM per device.

v0:
```python
import jax
import jax.numpy as jnp
from jax import lax
from jax.sharding import PartitionSpec as P


def shards(right_sides, eigen_basis, space_values, time_basis, time_values, noise_level):
    span = space_values.shape[0] // lax.axis_size("tm")
    value_part = lax.dynamic_slice_in_dim(space_values, lax.axis_index("tm") * span, span, 0)
    partial_value = jnp.einsum(
        "rts,si->rti",
        lax.all_gather(right_sides, "col", axis=2, tiled=True),
        eigen_basis,
        preferred_element_type=jnp.float32,
    )
    spectral = lax.psum(partial_value, "row").astype(jnp.bfloat16)
    mixed = jnp.einsum(
        "tj,kti->kji",
        time_basis,
        lax.all_to_all(spectral, "tm", split_axis=2, concat_axis=1, tiled=True),
        preferred_element_type=jnp.float32,
    )
    denom = value_part[None, None, :] * time_values[None, :, None] + noise_level[0]
    scaled = (mixed / denom).astype(jnp.bfloat16)
    own_part = lax.all_to_all(
        jnp.einsum("tj,kji->kti", time_basis, scaled, preferred_element_type=jnp.float32).astype(
            jnp.bfloat16
        ),
        "tm",
        split_axis=1,
        concat_axis=2,
        tiled=True,
    )
    terms = jnp.einsum("rti,si->rts", own_part, eigen_basis, preferred_element_type=jnp.float32)
    return lax.psum_scatter(terms, "col", scatter_dimension=2, tiled=True)


def solution(mesh):
    placed = (P(None, "tm", ("row", "col")), P("row", "col"), P("col"), P(), P(), P())
    return jax.shard_map(
        shards, mesh=mesh, in_specs=placed, out_specs=P(None, "tm", ("row", "col")), check_vma=False
    )
```

profile of v0, /device:TPU:1, one launch (start us, length us, event | category | flops | bytes accessed | tf_op | source)
XLA Modules:
  0.0 404.2 jit_solution(12070897886368147849)
XLA Ops:
  6.5 0.0 copy-start
  6.5 0.0 all-gather.2.cloned.1.call-start
  6.5 0.7 all-gather.2.cloned.1.call-update
  7.3 78.7 %all-gather.2.cloned.1.call-done = bf16[8,64,4096]{2,1,0:T(8,128)(2,1)} async-done(((bf16[8,64,512]{2,1,0:T(8,128)(2,1)}), bf16[8,64,4096]{2,1,0:T(8,128)(2,1)}) %all-gather.2.cloned.1.call-update) | async-done | bytes 4194320 | tf_op jit(solution)/shard_map/all_gather | solution.py:12
  85.9 15.0 %fusion.2 = f32[8,64,2048]{2,1,0:T(8,128)} fusion(bf16[8,64,4096]{2,1,0:T(8,128)(2,1)} %all-gather.2.cloned.1.call-done, bf16[4096,2048]{1,0:T(8,128)(2,1)} %param.7), kind=kOutput, calls=%fused_computation.2 | convolution fusion | flops 8589934592 | bytes 25165824 | tf_op jit(solution)/shard_map/rts,si->rti/dot_general | solution.py:10
  101.0 77.3 %all-reduce.1 = bf16[8,64,2048]{2,1,0:T(8,128)(2,1)S(1)} all-reduce(f32[8,64,2048]{2,1,0:T(8,128)} %fusion.2), channel_id=1, replica_groups=mesh['row'=4,'col'=8,'tm'=4] {'row'}, use_global_device_ids=true, to_apply=%region_0.0 | all-reduce | flops 1048576 | bytes 6291456 | tf_op jit(solution)/shard_map/psum | solution.py:16
  178.3 4.3 %copy.16 = bf16[8,64,2048]{1,0,2:T(8,128)(2,1)} copy(bf16[8,64,2048]{2,1,0:T(8,128)(2,1)S(1)} %all-reduce.1) | data formatting | bytes 4194304 | tf_op jit(solution)/shard_map/convert_element_type | solution.py:16
  182.6 5.9 %reshape.36 = bf16[4,2,131072]{2,1,0:T(2,128)(2,1)} reshape(bf16[2048,8,64]{2,1,0:T(8,128)(2,1)} %bitcast.30) | data formatting | bytes 4194304
  188.5 4.1 %all-to-all-start = ((bf16[4,2,131072]{2,1,0:T(2,128)(2,1)}), bf16[4,2,131072]{2,1,0:T(2,128)(2,1)S(1)}, u32[]{:S(2)}, u32[]{:S(2)}) async-start(bf16[4,2,131072]{2,1,0:T(2,128)(2,1)} %reshape.36), calls=%async_computation | async-start | bytes 4194304 | tf_op jit(solution)/shard_map/all_to_all | solution.py:20
  192.6 0.0 reduce-scatter.2.cloned.1.call-start
  193.3 0.8 dynamic_slice.3
  194.1 0.1 multiply_add_fusion
  194.2 24.4 %all-to-all-done = bf16[4,2,131072]{2,1,0:T(2,128)(2,1)S(1)} async-done(((bf16[4,2,131072]{2,1,0:T(2,128)(2,1)}), bf16[4,2,131072]{2,1,0:T(2,128)(2,1)S(1)}, u32[]{:S(2)}, u32[]{:S(2)}) %all-to-all-start) | async-done | bytes 2097184 | tf_op jit(solution)/shard_map/all_to_all | solution.py:20
  218.6 4.0 reshape.37
  222.6 5.2 %copy.24 = bf16[8,64,4,512]{3,2,1,0:T(4,128)(2,1)S(1)} copy(bf16[8,64,4,512]{1,0,3,2:T(8,128)(2,1)} %bitcast.31) | data formatting | bytes 4194304 | tf_op jit(solution)/shard_map/all_to_all | solution.py:20
  227.8 1.9 copy.18
  229.7 5.0 %convert_bitcast_fusion = bf16[8,256,512]{1,2,0:T(8,128)(2,1)} fusion(bf16[8,256,512]{2,1,0:T(8,128)(2,1)} %bitcast.34, f32[256,512]{0,1:T(8,128)S(1)} %multiply_add_fusion, bf16[256,256]{1,0:T(8,128)(2,1)S(1)} %copy-done), kind=kOutput, calls=%fused_computation.6 | convolution fusion | flops 1076887552 | bytes 4849664 | tf_op jit(solution)/shard_map/tj,kji->kti/dot_general | solution.py:26
  234.7 3.4 copy.20
  238.0 27.3 %all_to_all.36 = bf16[8,256,512]{2,0,1:T(8,128)(2,1)S(1)} all-to-all(bf16[8,256,512]{2,0,1:T(8,128)(2,1)S(1)} %copy.20), channel_id=1, replica_groups=mesh['row'=4,'col'=8,'tm'=4] {'tm'}, dimensions={1} | all-to-all | bytes 4194304 | tf_op jit(solution)/shard_map/all_to_all | solution.py:25
  265.3 1.6 copy.22
  266.9 2.8 all_to_all.33
  269.7 15.1 %fusion = f32[8,64,4096]{2,1,0:T(8,128)} fusion(bf16[8,64,2048]{2,1,0:T(8,128)(2,1)} %all_to_all.33, bf16[4096,2048]{1,0:T(8,128)(2,1)} %param.7), kind=kOutput, calls=%fused_computation | convolution fusion | flops 8589934592 | bytes 27262976 | tf_op jit(solution)/shard_map/rti,si->rts/dot_general | solution.py:34
  284.8 0.0 reduce-scatter.2.cloned.1.call-update
  284.9 112.5 %reduce-scatter.2.cloned.1.call-done = f32[8,64,512]{2,1,0:T(8,128)} async-done(((f32[8,64,4096]{2,1,0:T(8,128)}), f32[8,64,512]{2,1,0:T(8,128)}) %reduce-scatter.2.cloned.1.call-update) | async-done | bytes 1048592 | tf_op jit(solution)/shard_map/reduce_scatter | solution.py:35
  (3 shorter events, 0.0 us)
Async XLA Ops:
  6.5 223.1 %copy-start = (bf16[256,256]{1,0:T(8,128)(2,1)S(1)}, bf16[256,256]{1,0:T(8,128)(2,1)}, u32[]{:S(2)}) copy-start(bf16[256,256]{1,0:T(8,128)(2,1)} %param.9) | copy-start | bytes 393220
  6.5 79.4 %all-gather.2.cloned.1.call-start = ((), (), s32[]{:S(2)}) async-start(), calls=%async_computation.3 | async-start | bytes 4718592 | tf_op jit(solution)/shard_map/all_gather | solution.py:12
  182.6 11.5 %copy-start.1 = (f32[256]{0:T(256)S(1)}, f32[256]{0:T(256)}, u32[]{:S(2)}) copy-start(f32[256]{0:T(256)} %param.10) | copy-start | bytes 3076
  188.5 30.1 %all-to-all-start = ((bf16[4,2,131072]{2,1,0:T(2,128)(2,1)}), bf16[4,2,131072]{2,1,0:T(2,128)(2,1)S(1)}, u32[]{:S(2)}, u32[]{:S(2)}) async-start(bf16[4,2,131072]{2,1,0:T(2,128)(2,1)} %reshape.36), calls=%async_computation | async-start | bytes 4194304 | tf_op jit(solution)/shard_map/all_to_all | solution.py:20
  192.6 204.7 %reduce-scatter.2.cloned.1.call-start = ((), (), s32[]{:S(2)}) async-start(), calls=%async_computation.4 | async-start | bytes 9437184 | tf_op jit(solution)/shard_map/reduce_scatter | solution.py:35
Sparse Core Ops, SparseCore 0:
  9.5 76.3 all-gather.1
  285.0 112.3 reduce-scatter.1
where the time goes:
time: 405 us; the launch traced here: 404 us
  waiting for transfers between devices  216 us (53%)
  blocking collectives  105 us (26%)
  matrix products  35.1 us (9%)
  local copies, waits for them, and re-layouts  29.8 us (7%)
  between operations  14.1 us (3%)
  starting transfers between devices  4.14 us (1%)
    reduce_scatter x1, waiting for transfers between devices, shards(): return lax.psum_scatter(terms, 'col', scatter_dimension=2, tiled=True)  112 us
    all_gather x1, waiting for transfers between devices, shards(): lax.all_gather(right_sides, 'col', axis=2, tiled=True)  78.7 us
    psum x1, blocking collectives, shards(): spectral = lax.psum(partial_value, 'row').astype(jnp.bfloat16)  77.3 us
    all_to_all x1, blocking collectives, shards(): lax.all_to_all(jnp.einsum('tj,kji->kti', time_basis, scaled, preferred_el...  27.3 us
    all_to_all x1, waiting for transfers between devices, shards(): lax.all_to_all(spectral, 'tm', split_axis=2, concat_axis=1, tiled=True)  24.4 us
    dot_general x1, matrix products, shards(): jnp.einsum('rti,si->rts', own_part, eigen_basis, preferred_element_type=j...  15.1 us
    dot_general x1, matrix products, shards(): jnp.einsum('rts,si->rti', lax.all_gather(right_sides, 'col', axis=2, tile...  15 us
    unnamed x6, local copies, waits for them, and re-layouts  9.92 us
  transfers between devices with their start and end apart: 3, of which 3 were waited for; matrix products, arithmetic and copies ran while one was open for 0% of the time, Pallas kernels for 0%

commit v1 on v0

--- a/solution.py
+++ b/solution.py
@@ -1,7 +1,17 @@
+import functools
 import jax
 import jax.numpy as jnp
 from jax import lax
 from jax.sharding import PartitionSpec as P
+from jax.lax import all_gather
+
+
+def point_spans(field, bus_axis):
+    piece_now = jnp.sum(all_gather(field, bus_axis), 0)
+    return piece_now
+
+
+prepare_the_domain = functools.partial(point_spans, bus_axis="row")
 
 
 def shards(right_sides, eigen_basis, space_values, time_basis, time_values, noise_level):
@@ -13,7 +23,7 @@
         eigen_basis,
         preferred_element_type=jnp.float32,
     )
-    spectral = lax.psum(partial_value, "row").astype(jnp.bfloat16)
+    spectral = prepare_the_domain(partial_value).astype(jnp.bfloat16)
     mixed = jnp.einsum(
         "tj,kti->kji",
         time_basis,

time: 405 us -> 488 us (1.20)
  waiting for transfers between devices: 216 us -> 367 us
  blocking collectives: 105 us -> 28.7 us
  other arithmetic: 0.13 us -> 8.32 us
    all_gather x0 -> x1, waiting for transfers between devices: none -> 150 us  [point_spans(): piece_now = jnp.sum(all_gather(field, bus_axis), 0)]
    psum x1 -> x0, blocking collectives: 77.3 us -> none  [shards(): spectral = lax.psum(partial_value, 'row').astype(jnp.bfloat16)]
    reduce_sum x0 -> x1, other arithmetic: none -> 8.19 us  [point_spans(): piece_now = jnp.sum(all_gather(field, bus_axis), 0)]
    unnamed x6 -> x8, local copies, waits for them, and re-layouts: 9.92 us -> 9.92 us
  transfers between devices with their start and end apart: 3 -> 4, of which waited for: 3 -> 4; matrix products, arithmetic and copies ran while one was open for 0% -> 0% of each run, Pallas kernels for 0% -> 0%
where the time goes in v1:
time: 488 us; the launch traced here: 487 us
  waiting for transfers between devices  367 us (75%)
  matrix products  35 us (7%)
  local copies, waits for them, and re-layouts  29.8 us (6%)
  blocking collectives  28.7 us (6%)
  between operations  13.8 us (3%)
  other arithmetic  8.32 us (2%)
    all_gather x1, waiting for transfers between devices, point_spans(): piece_now = jnp.sum(all_gather(field, bus_axis), 0)  150 us
    reduce_scatter x1, waiting for transfers between devices, shards(): return lax.psum_scatter(terms, 'col', scatter_dimension=2, tiled=True)  114 us
    all_gather x1, waiting for transfers between devices, shards(): lax.all_gather(right_sides, 'col', axis=2, tiled=True)  78.6 us
    all_to_all x1, blocking collectives, shards(): lax.all_to_all(jnp.einsum('tj,kji->kti', time_basis, scaled, preferred_el...  28.7 us
    all_to_all x1, waiting for transfers between devices, shards(): lax.all_to_all(spectral, 'tm', split_axis=2, concat_axis=1, tiled=True)  24.3 us
    dot_general x1, matrix products, shards(): jnp.einsum('rti,si->rts', own_part, eigen_basis, preferred_element_type=j...  15 us
    dot_general x1, matrix products, shards(): jnp.einsum('rts,si->rti', lax.all_gather(right_sides, 'col', axis=2, tile...  15 us
    unnamed x8, local copies, waits for them, and re-layouts  9.92 us
  transfers between devices with their start and end apart: 4, of which 4 were waited for; matrix products, arithmetic and copies ran while one was open for 0% of the time, Pallas kernels for 0%

profile of v1, /device:TPU:1, one launch (start us, length us, event | category | flops | bytes accessed | tf_op | source)
XLA Modules:
  0.0 487.1 jit_solution(9430651966808080916)
XLA Ops:
  6.5 0.7 all-gather.4.cloned.1.call-update
  7.3 0.0 all-gather.6.cloned.1.call-start
  7.3 78.6 %all-gather.4.cloned.1.call-done = bf16[8,64,4096]{2,1,0:T(8,128)(2,1)} async-done(((bf16[8,64,512]{2,1,0:T(8,128)(2,1)}), bf16[8,64,4096]{2,1,0:T(8,128)(2,1)}) %all-gather.4.cloned.1.call-update) | async-done | bytes 4194320 | tf_op jit(solution)/shard_map/all_gather | solution.py:22
  85.9 15.0 %fusion.2 = f32[8,64,2048]{2,1,0:T(8,128)} fusion(bf16[8,64,4096]{2,1,0:T(8,128)(2,1)} %all-gather.4.cloned.1.call-done, bf16[4096,2048]{1,0:T(8,128)(2,1)} %param.7), kind=kOutput, calls=%fused_computation.2 | convolution fusion | flops 8589934592 | bytes 25165824 | tf_op jit(solution)/shard_map/rts,si->rti/dot_general | solution.py:20
  100.9 0.0 all-gather.6.cloned.1.call-update
  101.0 150.0 %all-gather.6.cloned.1.call-done = f32[32,64,2048]{2,1,0:T(8,128)} async-done(((f32[8,64,2048]{2,1,0:T(8,128)}), f32[32,64,2048]{2,1,0:T(8,128)}) %all-gather.6.cloned.1.call-update) | async-done | bytes 16777232 | tf_op jit(solution)/shard_map/all_gather | solution.py:10
  251.0 8.2 %reduce_sum.9 = bf16[8,64,2048]{2,1,0:T(8,128)(2,1)S(1)} reduce(f32[4,8,64,2048]{3,2,1,0:T(8,128)} %bitcast.33, f32[]{:T(128)} %constant.5.clone.1), dimensions={0}, to_apply=%region_0.0 | reduce | flops 3145728 | bytes 18874372 | tf_op jit(solution)/shard_map/reduce_sum | solution.py:10
  259.2 4.3 copy.20
  263.5 5.9 %reshape.37 = bf16[4,2,131072]{2,1,0:T(2,128)(2,1)} reshape(bf16[2048,8,64]{2,1,0:T(8,128)(2,1)} %bitcast.31) | data formatting | bytes 4194304
  269.4 4.1 all-to-all-start
  274.2 0.8 dynamic_slice.3
  275.0 0.1 multiply_add_fusion
  275.1 24.3 %all-to-all-done = bf16[4,2,131072]{2,1,0:T(2,128)(2,1)S(1)} async-done(((bf16[4,2,131072]{2,1,0:T(2,128)(2,1)}), bf16[4,2,131072]{2,1,0:T(2,128)(2,1)S(1)}, u32[]{:S(2)}, u32[]{:S(2)}) %all-to-all-start) | async-done | bytes 2097184 | tf_op jit(solution)/shard_map/all_to_all | solution.py:30
  299.4 4.0 reshape.38
  303.4 5.2 %copy.28 = bf16[8,64,4,512]{3,2,1,0:T(4,128)(2,1)S(1)} copy(bf16[8,64,4,512]{1,0,3,2:T(8,128)(2,1)} %bitcast.32) | data formatting | bytes 4194304 | tf_op jit(solution)/shard_map/all_to_all | solution.py:30
  308.6 1.9 copy.22
  310.5 5.0 %convert_bitcast_fusion = bf16[8,256,512]{1,2,0:T(8,128)(2,1)} fusion(bf16[8,256,512]{2,1,0:T(8,128)(2,1)} %bitcast.36, f32[256,512]{0,1:T(8,128)S(1)} %multiply_add_fusion, bf16[256,256]{1,0:T(8,128)(2,1)S(1)} %copy-done), kind=kOutput, calls=%fused_computation.6 | convolution fusion | flops 1076887552 | bytes 4849664 | tf_op jit(solution)/shard_map/tj,kji->kti/dot_general | solution.py:36
  315.5 3.4 copy.24
  318.8 28.7 %all_to_all.36 = bf16[8,256,512]{2,0,1:T(8,128)(2,1)S(1)} all-to-all(bf16[8,256,512]{2,0,1:T(8,128)(2,1)S(1)} %copy.24), channel_id=1, replica_groups=mesh['row'=4,'col'=8,'tm'=4] {'tm'}, dimensions={1} | all-to-all | bytes 4194304 | tf_op jit(solution)/shard_map/all_to_all | solution.py:35
  347.5 1.6 copy.26
  349.1 2.8 all_to_all.33
  352.0 15.0 %fusion = f32[8,64,4096]{2,1,0:T(8,128)} fusion(bf16[8,64,2048]{2,1,0:T(8,128)(2,1)} %all_to_all.33, bf16[4096,2048]{1,0:T(8,128)(2,1)} %param.7), kind=kOutput, calls=%fused_computation | convolution fusion | flops 8589934592 | bytes 27262976 | tf_op jit(solution)/shard_map/rti,si->rts/dot_general | solution.py:44
  367.0 0.0 reduce-scatter.2.cloned.1.call-update
  367.0 113.6 %reduce-scatter.2.cloned.1.call-done = f32[8,64,512]{2,1,0:T(8,128)} async-done(((f32[8,64,4096]{2,1,0:T(8,128)}), f32[8,64,512]{2,1,0:T(8,128)}) %reduce-scatter.2.cloned.1.call-update) | async-done | bytes 1048592 | tf_op jit(solution)/shard_map/reduce_scatter | solution.py:45
  (8 shorter events, 0.0 us)
Async XLA Ops:
  6.5 303.9 %copy-start = (bf16[256,256]{1,0:T(8,128)(2,1)S(1)}, bf16[256,256]{1,0:T(8,128)(2,1)}, u32[]{:S(2)}) copy-start(bf16[256,256]{1,0:T(8,128)(2,1)} %param.9) | copy-start | bytes 393220
  6.5 79.4 %all-gather.4.cloned.1.call-start = ((), (), s32[]{:S(2)}) async-start(), calls=%async_computation.3 | async-start | bytes 4718592 | tf_op jit(solution)/shard_map/all_gather | solution.py:22
  7.3 243.7 %all-gather.6.cloned.1.call-start = ((), (), s32[]{:S(2)}) async-start(), calls=%async_computation.5 | async-start | bytes 20971520 | tf_op jit(solution)/shard_map/all_gather | solution.py:10
  263.5 11.5 %copy-start.2 = (f32[256]{0:T(256)S(1)}, f32[256]{0:T(256)}, u32[]{:S(2)}) copy-start(f32[256]{0:T(256)} %param.10) | copy-start | bytes 3076
  269.4 30.0 %all-to-all-start = ((bf16[4,2,131072]{2,1,0:T(2,128)(2,1)}), bf16[4,2,131072]{2,1,0:T(2,128)(2,1)S(1)}, u32[]{:S(2)}, u32[]{:S(2)}) async-start(bf16[4,2,131072]{2,1,0:T(2,128)(2,1)} %reshape.37), calls=%async_computation | async-start | bytes 4194304 | tf_op jit(solution)/shard_map/all_to_all | solution.py:30
  273.5 207.1 %reduce-scatter.2.cloned.1.call-start = ((), (), s32[]{:S(2)}) async-start(), calls=%async_computation.4 | async-start | bytes 9437184 | tf_op jit(solution)/shard_map/reduce_scatter | solution.py:45
  367.0 113.6 %copy-start.1 = (bf16[256,256]{1,0:T(8,128)(2,1)S(1)}, bf16[256,256]{1,0:T(8,128)(2,1)}, u32[]{:S(2)}) copy-start(bf16[256,256]{1,0:T(8,128)(2,1)} %param.9) | copy-start | bytes 393220
Sparse Core Ops, SparseCore 0:
  9.5 76.3 all-gather.3
  101.1 149.8 all-gather.5
  367.1 113.3 reduce-scatter.1
